TPU v7x, 256 devices: a whole 4x4x8 slice. The times are simulated.
256 devices in a mesh: section: 8 (over x, core), blk: 32 (over y, z).
Axes of the slice: x: 4, y: 4, z: 8, core: 2. Of those that a mesh axis runs over, the one named last changes fastest.
Arguments:
- hidden: bfloat16 [16384, 1536], P('blk'), may hold values from -6 to 6
- stale_kv: bfloat16 [8, 16384, 3072], P('section', 'blk'), may hold values from -6 to 6
- w_qkv: bfloat16 [8, 1536, 4608], P('section', 'blk'), may hold values from -0.15625 to 0.15625
- w_out: bfloat16 [8, 1536, 1536], P('section', 'blk'), may hold values from -0.15625 to 0.15625
- q_gain: float32 [8, 128], P('section'), may hold values from 0.25 to 1.75
- k_gain: float32 [8, 128], P('section'), may hold values from 0.25 to 1.75
- mod_table: float32 [8, 16, 3, 1536], P('section'), may hold values from -4 to 4
- pattern: int32 [128, 8], P('blk'), may hold values from 0 to 1, as said below
- step_index: int32 [128], P('blk'), may hold values from 0 to 15
- order: int32 [4], replicated, may hold values from 0 to 3, each once
Outputs:
- layer_out: bfloat16 [8, 16384, 1536], P('section', 'blk')
- kv_cache: bfloat16 [8, 16384, 3072], P('section', 'blk')
Inputs may be any that keep to these rules, and one draw needn't show every extreme that they name: `pattern`: every row of the query tile's own tile (candidate c = tile index mod 4) is 1. `order`: names each patch once.
All inputs are finite; a program needn't handle non-finite values.
Results may differ from a plain program's by a relative error of at most 0.01.
Values may be sent and summed in bfloat16 or wider, within the bound.
A program may use at most 128 MiB of HBM per device.

v0:
```python
import math
import jax
import jax.numpy as jnp
from jax import lax
from jax.sharding import PartitionSpec as P

D = 1536
HEADS = 12
HDIM = 128
TILE = 128
PATCHES = 4
TSTEPS = 16
TOK_DEV = 128
NORM_EPS = 1e-06


def shifted(value, axis, steps):
    count = lax.axis_size(axis)
    pairs = [(source, (source + steps) % count) for source in range(count)]
    return lax.ppermute(value, axis, pairs)


def shifted_2(x, axis, by):
    count = lax.axis_size(axis)
    pairs = [(i, i + by) for i in range(count) if 0 <= i + by < count]
    return lax.ppermute(x, axis, pairs)


def layer_norm(values):
    centre = values - jnp.mean(values, axis=-1, keepdims=True)
    spread = jnp.mean(centre * centre, axis=-1, keepdims=True)
    return centre * lax.rsqrt(spread + NORM_EPS)


def head_norm(values, gain_row):
    square = jnp.mean(values * values, axis=-1, keepdims=True)
    return values * lax.rsqrt(square + NORM_EPS) * gain_row


def on_device(
    hidden, stale_kv, w_qkv, w_out, q_gain, k_gain, mod_table, pattern, step_index, order
):
    inner_width = HEADS * HDIM
    rows_patch = TOK_DEV
    tiles_patch = rows_patch // TILE
    candidate_tiles = pattern.shape[1]
    sections = lax.axis_size("section")
    section_id = lax.axis_index("section")
    full_qkv, full_out = (
        lax.all_gather(w_qkv[0], "blk", axis=0, tiled=True),
        lax.all_gather(w_out[0], "blk", axis=0, tiled=True),
    )
    query_gain = q_gain[0]
    key_gain = k_gain[0]
    modulation_table = mod_table[0].reshape(TSTEPS, 3 * D)
    tile_masks = pattern.reshape(PATCHES, tiles_patch, candidate_tiles)
    steps_tiles = step_index.reshape(PATCHES, tiles_patch)
    input_rows = hidden.reshape(PATCHES, rows_patch, D)
    own_store = stale_kv[0].reshape(PATCHES, rows_patch, 2 * inner_width)
    near_store = shifted(own_store, "blk", 1)
    received = jnp.zeros((rows_patch, D), jnp.bfloat16)
    results = jnp.zeros((PATCHES, rows_patch, D), jnp.bfloat16)
    inverse_root = 1.0 / math.sqrt(HDIM)

    def slot_step(slot, state_now):
        received, own_store, near_store, results = state_now
        offset = slot - section_id
        active = jnp.logical_and(offset >= 0, offset < PATCHES)
        clipped = jnp.clip(offset, 0, PATCHES - 1)
        patch_id = jnp.sum(jnp.where(jnp.arange(PATCHES) == clipped, order, 0))
        tokens = jnp.where(
            section_id == 0,
            lax.dynamic_index_in_dim(input_rows, patch_id, 0, keepdims=False),
            received,
        )
        tile_steps = lax.dynamic_index_in_dim(steps_tiles, patch_id, 0, keepdims=False)
        one_hot = (tile_steps[:, None] == jnp.arange(TSTEPS)[None, :]).astype(jnp.float32)
        modulation = jnp.dot(one_hot, modulation_table, precision=lax.Precision.HIGHEST)
        modulation = jnp.broadcast_to(modulation[:, None, :], (tiles_patch, TILE, 3 * D)).reshape(
            rows_patch, 3 * D
        )
        shift_term = modulation[:, :D]
        scale_term = modulation[:, D : 2 * D]
        gate_term = modulation[:, 2 * D :]

        def project(token_rows):
            modulated = (
                layer_norm(token_rows.astype(jnp.float32)) * (1.0 + scale_term) + shift_term
            ).astype(jnp.bfloat16)
            qkv = jnp.dot(modulated, full_qkv, preferred_element_type=jnp.float32)
            queries = head_norm(
                qkv[:, :inner_width].reshape(rows_patch, HEADS, HDIM), query_gain
            ).astype(jnp.bfloat16)
            return (modulated, queries, qkv[:, inner_width:].astype(jnp.bfloat16))

        def spare_project(token_rows):
            return (
                jnp.zeros((rows_patch, D), jnp.bfloat16),
                jnp.zeros((rows_patch, HEADS, HDIM), jnp.bfloat16),
                jnp.zeros((rows_patch, 2 * inner_width), jnp.bfloat16),
            )

        modulated, queries, fresh_kv = lax.cond(active, project, spare_project, tokens)
        own_store = jnp.where(
            active, lax.dynamic_update_index_in_dim(own_store, fresh_kv, patch_id, 0), own_store
        )
        near_fresh = shifted(fresh_kv, "blk", 1)
        near_store = jnp.where(
            active, lax.dynamic_update_index_in_dim(near_store, near_fresh, patch_id, 0), near_store
        )
        tile_mask = lax.dynamic_index_in_dim(tile_masks, patch_id, 0, keepdims=False)

        def attend(operands):
            token_rows, query_rows, own_rows, near_rows = operands
            candidates = jnp.concatenate(
                [own_rows.reshape(-1, 2 * inner_width), near_rows.reshape(-1, 2 * inner_width)],
                axis=0,
            )
            key_rows = head_norm(
                candidates[:, :inner_width].astype(jnp.float32).reshape(-1, HEADS, HDIM), key_gain
            ).astype(jnp.bfloat16)
            value_rows = candidates[:, inner_width:].reshape(-1, HEADS, HDIM)
            token_mask = jnp.broadcast_to(
                tile_mask.astype(jnp.float32)[:, None, :, None],
                (tiles_patch, TILE, candidate_tiles, TILE),
            ).reshape(rows_patch, candidate_tiles * TILE)
            scores = (
                jnp.einsum("qhd,khd->hqk", query_rows, key_rows, preferred_element_type=jnp.float32)
                * inverse_root
            )
            expo = jnp.exp(scores) * token_mask[None]
            weight_sum = jnp.sum(expo, axis=-1)
            mixture = jnp.einsum(
                "hqk,khd->qhd",
                expo.astype(jnp.bfloat16),
                value_rows,
                preferred_element_type=jnp.float32,
            )
            attended = (
                (mixture / jnp.transpose(weight_sum)[:, :, None])
                .reshape(rows_patch, inner_width)
                .astype(jnp.bfloat16)
            )
            projected = jnp.dot(attended, full_out, preferred_element_type=jnp.float32)
            return (token_rows.astype(jnp.float32) + gate_term * projected).astype(jnp.bfloat16)

        def spare_attend(operands):
            return jnp.zeros((rows_patch, D), jnp.bfloat16)

        output_rows = lax.cond(
            active, attend, spare_attend, (tokens, queries, own_store, near_store)
        )
        results = jnp.where(
            active, lax.dynamic_update_index_in_dim(results, output_rows, patch_id, 0), results
        )
        received = shifted_2(output_rows, "section", 1)
        return (received, own_store, near_store, results)

    slot_count = PATCHES + sections - 1
    received, own_store, near_store, results = lax.fori_loop(
        0, slot_count, slot_step, (received, own_store, near_store, results)
    )
    layer_out = results.reshape(1, PATCHES * rows_patch, D)
    kv_cache = own_store.reshape(1, PATCHES * rows_patch, 2 * inner_width)
    return (layer_out, kv_cache)


def solution(mesh):
    in_specs = (
        P("blk", None),
        P("section", "blk", None),
        P("section", "blk", None),
        P("section", "blk", None),
        P("section", None),
        P("section", None),
        P("section", None, None, None),
        P("blk", None),
        P("blk"),
        P(),
    )
    out_specs = (P("section", "blk", None), P("section", "blk", None))
    return jax.shard_map(
        on_device, mesh=mesh, in_specs=in_specs, out_specs=out_specs, check_vma=False
    )
```

profile of v0, /device:TPU:7, one launch (start us, length us, event | category | flops | bytes accessed | tf_op | source)
XLA Modules:
  0.0 1030.1 jit_solution(15740919164373035649)
XLA Ops:
  7.2 3.8 copy.63
  14.6 101.2 %collective-permute-done.2 = bf16[4,128,3072]{2,1,0:T(8,128)(2,1)} collective-permute-done((bf16[4,128,3072]{2,1,0:T(8,128)(2,1)}, bf16[4,128,3072]{2,1,0:T(8,128)(2,1)}, u32[]{:S(2)}, u32[]{:S(2)}) %collective-permute-start.2) | collective-permute-done | bytes 3145760 | tf_op jit(solution)/shard_map/ppermute | solution.py:20
  115.7 125.9 %all-gather.5.cloned.1.call-done = bf16[1,1536,4608]{2,1,0:T(8,128)(2,1)} async-done(((bf16[1,48,4608]{2,1,0:T(8,128)(2,1)}), bf16[1,1536,4608]{2,1,0:T(8,128)(2,1)}) %all-gather.5.cloned.1.call-update) | async-done | bytes 14155792 | tf_op jit(solution)/shard_map/all_gather | solution.py:50
  242.9 780.4 %while.20 = (s32[]{:T(128)}, bf16[128,1536]{1,0:T(8,128)(2,1)S(1)}, bf16[4,128,3072]{2,1,0:T(8,128)(2,1)}, bf16[4,128,3072]{2,1,0:T(8,128)(2,1)}, bf16[4,128,153...) while((s32[]{:T(128)}, bf16[128,1536]{1,0:T(8,128)(2,1)S(1)}, ...), condition=%wide.region_11.12_spmd, body=%wide.region_0.11_spmd.sunk | while | flops 3260855808 | bytes 107183792 | solution.py:160
  249.5 2.8 conditional.4
  254.6 19.3 %collective-permute-done = bf16[128,3072]{1,0:T(8,128)(2,1)S(1)} collective-permute-done((bf16[128,3072]{1,0:T(8,128)(2,1)}, bf16[128,3072]{1,0:T(8,128)(2,1)S(1)}, u32[]{:S(2)}, u32[]{:S(2)}) %collective-permute-start) | collective-permute-done | bytes 786464 | tf_op jit(solution)/shard_map/while/body/eval_jaxpr/ppermute | solution.py:20
  286.1 2.4 convolution_reduce_fusion.2
  289.5 2.8 conditional.4
  294.6 14.4 %collective-permute-done = bf16[128,3072]{1,0:T(8,128)(2,1)S(1)} collective-permute-done((bf16[128,3072]{1,0:T(8,128)(2,1)}, bf16[128,3072]{1,0:T(8,128)(2,1)S(1)}, u32[]{:S(2)}, u32[]{:S(2)}) %collective-permute-start) | collective-permute-done | bytes 786464 | tf_op jit(solution)/shard_map/while/body/eval_jaxpr/ppermute | solution.py:20
  315.9 7.1 collective-permute-done.1
  329.5 2.8 conditional.4
  334.6 13.3 %collective-permute-done = bf16[128,3072]{1,0:T(8,128)(2,1)S(1)} collective-permute-done((bf16[128,3072]{1,0:T(8,128)(2,1)}, bf16[128,3072]{1,0:T(8,128)(2,1)S(1)}, u32[]{:S(2)}, u32[]{:S(2)}) %collective-permute-start) | collective-permute-done | bytes 786464 | tf_op jit(solution)/shard_map/while/body/eval_jaxpr/ppermute | solution.py:20
  354.8 8.2 collective-permute-done.1
  369.5 2.8 conditional.4
  374.6 14.4 %collective-permute-done = bf16[128,3072]{1,0:T(8,128)(2,1)S(1)} collective-permute-done((bf16[128,3072]{1,0:T(8,128)(2,1)}, bf16[128,3072]{1,0:T(8,128)(2,1)S(1)}, u32[]{:S(2)}, u32[]{:S(2)}) %collective-permute-start) | collective-permute-done | bytes 786464 | tf_op jit(solution)/shard_map/while/body/eval_jaxpr/ppermute | solution.py:20
  395.9 7.1 collective-permute-done.1
  409.5 2.8 conditional.4
  414.6 14.4 %collective-permute-done = bf16[128,3072]{1,0:T(8,128)(2,1)S(1)} collective-permute-done((bf16[128,3072]{1,0:T(8,128)(2,1)}, bf16[128,3072]{1,0:T(8,128)(2,1)S(1)}, u32[]{:S(2)}, u32[]{:S(2)}) %collective-permute-start) | collective-permute-done | bytes 786464 | tf_op jit(solution)/shard_map/while/body/eval_jaxpr/ppermute | solution.py:20
  435.9 7.1 collective-permute-done.1
  449.5 2.8 conditional.4
  454.6 14.4 %collective-permute-done = bf16[128,3072]{1,0:T(8,128)(2,1)S(1)} collective-permute-done((bf16[128,3072]{1,0:T(8,128)(2,1)}, bf16[128,3072]{1,0:T(8,128)(2,1)S(1)}, u32[]{:S(2)}, u32[]{:S(2)}) %collective-permute-start) | collective-permute-done | bytes 786464 | tf_op jit(solution)/shard_map/while/body/eval_jaxpr/ppermute | solution.py:20
  475.9 7.1 collective-permute-done.1
  489.5 2.8 conditional.4
  494.6 12.2 %collective-permute-done = bf16[128,3072]{1,0:T(8,128)(2,1)S(1)} collective-permute-done((bf16[128,3072]{1,0:T(8,128)(2,1)}, bf16[128,3072]{1,0:T(8,128)(2,1)S(1)}, u32[]{:S(2)}, u32[]{:S(2)}) %collective-permute-start) | collective-permute-done | bytes 786464 | tf_op jit(solution)/shard_map/while/body/eval_jaxpr/ppermute | solution.py:20
  513.7 209.5 %collective-permute-done.1 = bf16[128,1536]{1,0:T(8,128)(2,1)S(1)} collective-permute-done((bf16[128,1536]{1,0:T(8,128)(2,1)}, bf16[128,1536]{1,0:T(8,128)(2,1)S(1)}, u32[]{:S(2)}, u32[]{:S(2)}) %collective-permute-start.1) | collective-permute-done | bytes 393248 | tf_op jit(solution)/shard_map/while/body/eval_jaxpr/ppermute | solution.py:26
  729.7 13.7 %conditional.4 = (bf16[128,12,128]{0,2,1:T(8,128)(2,1)}, bf16[128,3072]{1,0:T(8,128)(2,1)}, bf16[1,128,3072]{2,1,0:T(8,128)(2,1)}) conditional(s32[]{:T(128)} %convert_element_type.92, () %tuple.70, (bf16[128,1536]{1,0:T(8,128)(2,1)S(1)}, f32[4608]{0:T(1024)}, bf16[1536,4608]{1,0:T(8,128)(2,1)}, f32[1,128]{1,0:T(1,128)S(1)}) %tuple.71), branch_computations={%region_2.2_spmd, %region_3.6_spmd} | conditional | flops 1815284864 | bytes 26018840 | solution.py:103
  730.9 7.1 fusion.6
  743.5 2.4 select_dynamic-update-slice_fusion.4
  745.9 11.9 %collective-permute-done = bf16[128,3072]{1,0:T(8,128)(2,1)S(1)} collective-permute-done((bf16[128,3072]{1,0:T(8,128)(2,1)}, bf16[128,3072]{1,0:T(8,128)(2,1)S(1)}, u32[]{:S(2)}, u32[]{:S(2)}) %collective-permute-start) | collective-permute-done | bytes 786464 | tf_op jit(solution)/shard_map/while/body/eval_jaxpr/ppermute | solution.py:20
  760.1 24.4 %conditional.5 = (bf16[128,1536]{1,0:T(8,128)(2,1)}, bf16[1,128,1536]{2,1,0:T(8,128)(2,1)}) conditional(s32[]{:T(128)} %convert_element_type.92, () %tuple.69, (bf16[128,1536]{1,0:T(8,128)(2,1)S(1)}, f32[4608]{0:T(1024)}, bf16[4,128,3072]{2,1,0:T(8,128)(2,1)}, bf16[4,128,3072]{2,1,0:T(8,128)(2,1)}, f32[1,128]{1,0:T(1,128)S(1)}, ...), branch_computations={%region_7.7_spmd, %region_8.10_spmd} | conditional | flops 1443506688 | bytes 69053088 | solution.py:150
  760.1 3.2 copy.32
  763.3 4.7 copy.31
  768.0 5.6 pad_maximum_fusion
  775.2 3.3 bitcast_reduce_fusion
  787.7 10.2 collective-permute-done.1
  804.5 13.7 %conditional.4 = (bf16[128,12,128]{0,2,1:T(8,128)(2,1)}, bf16[128,3072]{1,0:T(8,128)(2,1)}, bf16[1,128,3072]{2,1,0:T(8,128)(2,1)}) conditional(s32[]{:T(128)} %convert_element_type.92, () %tuple.70, (bf16[128,1536]{1,0:T(8,128)(2,1)S(1)}, f32[4608]{0:T(1024)}, bf16[1536,4608]{1,0:T(8,128)(2,1)}, f32[1,128]{1,0:T(1,128)S(1)}) %tuple.71), branch_computations={%region_2.2_spmd, %region_3.6_spmd} | conditional | flops 1815284864 | bytes 26018840 | solution.py:103
  805.7 7.1 fusion.6
  818.3 2.4 select_dynamic-update-slice_fusion.4
  820.7 11.9 %collective-permute-done = bf16[128,3072]{1,0:T(8,128)(2,1)S(1)} collective-permute-done((bf16[128,3072]{1,0:T(8,128)(2,1)}, bf16[128,3072]{1,0:T(8,128)(2,1)S(1)}, u32[]{:S(2)}, u32[]{:S(2)}) %collective-permute-start) | collective-permute-done | bytes 786464 | tf_op jit(solution)/shard_map/while/body/eval_jaxpr/ppermute | solution.py:20
  834.8 24.4 %conditional.5 = (bf16[128,1536]{1,0:T(8,128)(2,1)}, bf16[1,128,1536]{2,1,0:T(8,128)(2,1)}) conditional(s32[]{:T(128)} %convert_element_type.92, () %tuple.69, (bf16[128,1536]{1,0:T(8,128)(2,1)S(1)}, f32[4608]{0:T(1024)}, bf16[4,128,3072]{2,1,0:T(8,128)(2,1)}, bf16[4,128,3072]{2,1,0:T(8,128)(2,1)}, f32[1,128]{1,0:T(1,128)S(1)}, ...), branch_computations={%region_7.7_spmd, %region_8.10_spmd} | conditional | flops 1443506688 | bytes 69053088 | solution.py:150
  834.8 3.2 copy.32
  838.0 4.7 copy.31
  842.8 5.6 pad_maximum_fusion
  849.9 3.3 bitcast_reduce_fusion
  862.5 12.3 %collective-permute-done.1 = bf16[128,1536]{1,0:T(8,128)(2,1)S(1)} collective-permute-done((bf16[128,1536]{1,0:T(8,128)(2,1)}, bf16[128,1536]{1,0:T(8,128)(2,1)S(1)}, u32[]{:S(2)}, u32[]{:S(2)}) %collective-permute-start.1) | collective-permute-done | bytes 393248 | tf_op jit(solution)/shard_map/while/body/eval_jaxpr/ppermute | solution.py:26
  881.4 13.7 %conditional.4 = (bf16[128,12,128]{0,2,1:T(8,128)(2,1)}, bf16[128,3072]{1,0:T(8,128)(2,1)}, bf16[1,128,3072]{2,1,0:T(8,128)(2,1)}) conditional(s32[]{:T(128)} %convert_element_type.92, () %tuple.70, (bf16[128,1536]{1,0:T(8,128)(2,1)S(1)}, f32[4608]{0:T(1024)}, bf16[1536,4608]{1,0:T(8,128)(2,1)}, f32[1,128]{1,0:T(1,128)S(1)}) %tuple.71), branch_computations={%region_2.2_spmd, %region_3.6_spmd} | conditional | flops 1815284864 | bytes 26018840 | solution.py:103
  882.6 7.2 fusion.6
  895.2 2.4 select_dynamic-update-slice_fusion.4
  897.6 11.9 %collective-permute-done = bf16[128,3072]{1,0:T(8,128)(2,1)S(1)} collective-permute-done((bf16[128,3072]{1,0:T(8,128)(2,1)}, bf16[128,3072]{1,0:T(8,128)(2,1)S(1)}, u32[]{:S(2)}, u32[]{:S(2)}) %collective-permute-start) | collective-permute-done | bytes 786464 | tf_op jit(solution)/shard_map/while/body/eval_jaxpr/ppermute | solution.py:20
  911.7 24.4 %conditional.5 = (bf16[128,1536]{1,0:T(8,128)(2,1)}, bf16[1,128,1536]{2,1,0:T(8,128)(2,1)}) conditional(s32[]{:T(128)} %convert_element_type.92, () %tuple.69, (bf16[128,1536]{1,0:T(8,128)(2,1)S(1)}, f32[4608]{0:T(1024)}, bf16[4,128,3072]{2,1,0:T(8,128)(2,1)}, bf16[4,128,3072]{2,1,0:T(8,128)(2,1)}, f32[1,128]{1,0:T(1,128)S(1)}, ...), branch_computations={%region_7.7_spmd, %region_8.10_spmd} | conditional | flops 1443506688 | bytes 69053088 | solution.py:150
  911.7 3.2 copy.32
  914.9 4.7 copy.31
  919.7 5.6 pad_maximum_fusion
  926.8 3.3 bitcast_reduce_fusion
  939.4 14.8 %collective-permute-done.1 = bf16[128,1536]{1,0:T(8,128)(2,1)S(1)} collective-permute-done((bf16[128,1536]{1,0:T(8,128)(2,1)}, bf16[128,1536]{1,0:T(8,128)(2,1)S(1)}, u32[]{:S(2)}, u32[]{:S(2)}) %collective-permute-start.1) | collective-permute-done | bytes 393248 | tf_op jit(solution)/shard_map/while/body/eval_jaxpr/ppermute | solution.py:26
  960.8 13.7 %conditional.4 = (bf16[128,12,128]{0,2,1:T(8,128)(2,1)}, bf16[128,3072]{1,0:T(8,128)(2,1)}, bf16[1,128,3072]{2,1,0:T(8,128)(2,1)}) conditional(s32[]{:T(128)} %convert_element_type.92, () %tuple.70, (bf16[128,1536]{1,0:T(8,128)(2,1)S(1)}, f32[4608]{0:T(1024)}, bf16[1536,4608]{1,0:T(8,128)(2,1)}, f32[1,128]{1,0:T(1,128)S(1)}) %tuple.71), branch_computations={%region_2.2_spmd, %region_3.6_spmd} | conditional | flops 1815284864 | bytes 26018840 | solution.py:103
  962.0 7.1 fusion.6
  974.5 2.4 select_dynamic-update-slice_fusion.4
  977.0 15.9 %collective-permute-done = bf16[128,3072]{1,0:T(8,128)(2,1)S(1)} collective-permute-done((bf16[128,3072]{1,0:T(8,128)(2,1)}, bf16[128,3072]{1,0:T(8,128)(2,1)S(1)}, u32[]{:S(2)}, u32[]{:S(2)}) %collective-permute-start) | collective-permute-done | bytes 786464 | tf_op jit(solution)/shard_map/while/body/eval_jaxpr/ppermute | solution.py:20
  995.1 24.4 %conditional.5 = (bf16[128,1536]{1,0:T(8,128)(2,1)}, bf16[1,128,1536]{2,1,0:T(8,128)(2,1)}) conditional(s32[]{:T(128)} %convert_element_type.92, () %tuple.69, (bf16[128,1536]{1,0:T(8,128)(2,1)S(1)}, f32[4608]{0:T(1024)}, bf16[4,128,3072]{2,1,0:T(8,128)(2,1)}, bf16[4,128,3072]{2,1,0:T(8,128)(2,1)}, f32[1,128]{1,0:T(1,128)S(1)}, ...), branch_computations={%region_7.7_spmd, %region_8.10_spmd} | conditional | flops 1443506688 | bytes 69053088 | solution.py:150
  995.1 3.2 copy.32
  998.3 4.7 copy.31
  1003.0 5.6 pad_maximum_fusion
  1010.1 3.3 bitcast_reduce_fusion
  (258 shorter events, 229.7 us)
Async XLA Ops:
  7.2 6.4 copy-start
  7.2 108.6 %all-gather.7.cloned.1.call-start = ((), (), s32[]{:S(2)}) async-start(), calls=%async_computation.1 | async-start | bytes 4866048 | tf_op jit(solution)/shard_map/all_gather | solution.py:51
  11.0 231.9 %copy-start.1 = (f32[1,128]{1,0:T(1,128)S(1)}, f32[1,128]{1,0:T(1,128)}, u32[]{:S(2)}) copy-start(f32[1,128]{1,0:T(1,128)} %param.20) | copy-start | bytes 1540
  11.0 231.9 %copy-start.2 = (s32[4]{0:T(128)S(1)}, s32[4]{0:T(128)}, u32[]{:S(2)}) copy-start(s32[4]{0:T(128)} %param.25) | copy-start | bytes 52
  11.0 231.9 %copy-start.3 = (s32[4]{0:T(128)S(1)}, s32[4]{0:T(128)}, u32[]{:S(2)}) copy-start(s32[4]{0:T(128)} %param.24) | copy-start | bytes 52
  11.0 231.9 %copy-start.4 = (f32[1,128]{1,0:T(1,128)S(1)}, f32[1,128]{1,0:T(1,128)}, u32[]{:S(2)}) copy-start(f32[1,128]{1,0:T(1,128)} %param.21) | copy-start | bytes 1540
  11.0 230.5 %all-gather.5.cloned.1.call-start = ((), (), s32[]{:S(2)}) async-start(), calls=%async_computation | async-start | bytes 14598144 | tf_op jit(solution)/shard_map/all_gather | solution.py:50
  11.8 103.9 %collective-permute-start.2 = (bf16[4,128,3072]{2,1,0:T(8,128)(2,1)}, bf16[4,128,3072]{2,1,0:T(8,128)(2,1)}, u32[]{:S(2)}, u32[]{:S(2)}) collective-permute-start(bf16[4,128,3072]{2,1,0:T(8,128)(2,1)} %bitcast.20), channel_id=1, source_target_pairs={{0,1},{1,2},{2,3},{3,4},{4,5},{5,6},{6,7},{7,8},{8,9},{9,10},{10,1... | collective-permute-start | bytes 9437192 | tf_op jit(solution)/shard_map/ppermute | solution.py:20
  252.4 21.5 %collective-permute-start = (bf16[128,3072]{1,0:T(8,128)(2,1)}, bf16[128,3072]{1,0:T(8,128)(2,1)S(1)}, u32[]{:S(2)}, u32[]{:S(2)}) collective-permute-start(bf16[128,3072]{1,0:T(8,128)(2,1)} %get-tuple-element.585), channel_id=1, source_target_pairs={{0,1},{1,2},{2,3},{3,4},{4,5},{5,6},{6,7},{7,8},{8,9},{9,10},{10,1... | collective-permute-start | bytes 2359304 | tf_op jit(solution)/shard_map/while/body/eval_jaxpr/ppermute | solution.py:20
  277.7 5.3 collective-permute-start.1
  292.4 16.6 %collective-permute-start = (bf16[128,3072]{1,0:T(8,128)(2,1)}, bf16[128,3072]{1,0:T(8,128)(2,1)S(1)}, u32[]{:S(2)}, u32[]{:S(2)}) collective-permute-start(bf16[128,3072]{1,0:T(8,128)(2,1)} %get-tuple-element.585), channel_id=1, source_target_pairs={{0,1},{1,2},{2,3},{3,4},{4,5},{5,6},{6,7},{7,8},{8,9},{9,10},{10,1... | collective-permute-start | bytes 2359304 | tf_op jit(solution)/shard_map/while/body/eval_jaxpr/ppermute | solution.py:20
  312.7 10.2 collective-permute-start.1
  332.4 15.5 %collective-permute-start = (bf16[128,3072]{1,0:T(8,128)(2,1)}, bf16[128,3072]{1,0:T(8,128)(2,1)S(1)}, u32[]{:S(2)}, u32[]{:S(2)}) collective-permute-start(bf16[128,3072]{1,0:T(8,128)(2,1)} %get-tuple-element.585), channel_id=1, source_target_pairs={{0,1},{1,2},{2,3},{3,4},{4,5},{5,6},{6,7},{7,8},{8,9},{9,10},{10,1... | collective-permute-start | bytes 2359304 | tf_op jit(solution)/shard_map/while/body/eval_jaxpr/ppermute | solution.py:20
  351.6 11.3 %collective-permute-start.1 = (bf16[128,1536]{1,0:T(8,128)(2,1)}, bf16[128,1536]{1,0:T(8,128)(2,1)S(1)}, u32[]{:S(2)}, u32[]{:S(2)}) collective-permute-start(bf16[128,1536]{1,0:T(8,128)(2,1)} %get-tuple-element.587), channel_id=1, source_target_pairs={{0,32},{32,64},{64,96},{96,128},{128,160},{160,192},{192,224},{1,3... | collective-permute-start | bytes 1179656 | tf_op jit(solution)/shard_map/while/body/eval_jaxpr/ppermute | solution.py:26
  372.4 16.6 %collective-permute-start = (bf16[128,3072]{1,0:T(8,128)(2,1)}, bf16[128,3072]{1,0:T(8,128)(2,1)S(1)}, u32[]{:S(2)}, u32[]{:S(2)}) collective-permute-start(bf16[128,3072]{1,0:T(8,128)(2,1)} %get-tuple-element.585), channel_id=1, source_target_pairs={{0,1},{1,2},{2,3},{3,4},{4,5},{5,6},{6,7},{7,8},{8,9},{9,10},{10,1... | collective-permute-start | bytes 2359304 | tf_op jit(solution)/shard_map/while/body/eval_jaxpr/ppermute | solution.py:20
  392.7 10.2 collective-permute-start.1
  412.4 16.6 %collective-permute-start = (bf16[128,3072]{1,0:T(8,128)(2,1)}, bf16[128,3072]{1,0:T(8,128)(2,1)S(1)}, u32[]{:S(2)}, u32[]{:S(2)}) collective-permute-start(bf16[128,3072]{1,0:T(8,128)(2,1)} %get-tuple-element.585), channel_id=1, source_target_pairs={{0,1},{1,2},{2,3},{3,4},{4,5},{5,6},{6,7},{7,8},{8,9},{9,10},{10,1... | collective-permute-start | bytes 2359304 | tf_op jit(solution)/shard_map/while/body/eval_jaxpr/ppermute | solution.py:20
  432.7 10.2 collective-permute-start.1
  452.4 16.6 %collective-permute-start = (bf16[128,3072]{1,0:T(8,128)(2,1)}, bf16[128,3072]{1,0:T(8,128)(2,1)S(1)}, u32[]{:S(2)}, u32[]{:S(2)}) collective-permute-start(bf16[128,3072]{1,0:T(8,128)(2,1)} %get-tuple-element.585), channel_id=1, source_target_pairs={{0,1},{1,2},{2,3},{3,4},{4,5},{5,6},{6,7},{7,8},{8,9},{9,10},{10,1... | collective-permute-start | bytes 2359304 | tf_op jit(solution)/shard_map/while/body/eval_jaxpr/ppermute | solution.py:20
  472.7 10.2 collective-permute-start.1
  492.4 14.4 %collective-permute-start = (bf16[128,3072]{1,0:T(8,128)(2,1)}, bf16[128,3072]{1,0:T(8,128)(2,1)S(1)}, u32[]{:S(2)}, u32[]{:S(2)}) collective-permute-start(bf16[128,3072]{1,0:T(8,128)(2,1)} %get-tuple-element.585), channel_id=1, source_target_pairs={{0,1},{1,2},{2,3},{3,4},{4,5},{5,6},{6,7},{7,8},{8,9},{9,10},{10,1... | collective-permute-start | bytes 2359304 | tf_op jit(solution)/shard_map/while/body/eval_jaxpr/ppermute | solution.py:20
  510.5 212.6 %collective-permute-start.1 = (bf16[128,1536]{1,0:T(8,128)(2,1)}, bf16[128,1536]{1,0:T(8,128)(2,1)S(1)}, u32[]{:S(2)}, u32[]{:S(2)}) collective-permute-start(bf16[128,1536]{1,0:T(8,128)(2,1)} %get-tuple-element.587), channel_id=1, source_target_pairs={{0,32},{32,64},{64,96},{96,128},{128,160},{160,192},{192,224},{1,3... | collective-permute-start | bytes 1179656 | tf_op jit(solution)/shard_map/while/body/eval_jaxpr/ppermute | solution.py:26
  743.5 14.4 %collective-permute-start = (bf16[128,3072]{1,0:T(8,128)(2,1)}, bf16[128,3072]{1,0:T(8,128)(2,1)S(1)}, u32[]{:S(2)}, u32[]{:S(2)}) collective-permute-start(bf16[128,3072]{1,0:T(8,128)(2,1)} %get-tuple-element.585), channel_id=1, source_target_pairs={{0,1},{1,2},{2,3},{3,4},{4,5},{5,6},{6,7},{7,8},{8,9},{9,10},{10,1... | collective-permute-start | bytes 2359304 | tf_op jit(solution)/shard_map/while/body/eval_jaxpr/ppermute | solution.py:20
  775.1 6.0 slice-start
  778.5 2.7 slice-start.1
  784.5 13.5 %collective-permute-start.1 = (bf16[128,1536]{1,0:T(8,128)(2,1)}, bf16[128,1536]{1,0:T(8,128)(2,1)S(1)}, u32[]{:S(2)}, u32[]{:S(2)}) collective-permute-start(bf16[128,1536]{1,0:T(8,128)(2,1)} %get-tuple-element.587), channel_id=1, source_target_pairs={{0,32},{32,64},{64,96},{96,128},{128,160},{160,192},{192,224},{1,3... | collective-permute-start | bytes 1179656 | tf_op jit(solution)/shard_map/while/body/eval_jaxpr/ppermute | solution.py:26
  818.3 14.4 %collective-permute-start = (bf16[128,3072]{1,0:T(8,128)(2,1)}, bf16[128,3072]{1,0:T(8,128)(2,1)S(1)}, u32[]{:S(2)}, u32[]{:S(2)}) collective-permute-start(bf16[128,3072]{1,0:T(8,128)(2,1)} %get-tuple-element.585), channel_id=1, source_target_pairs={{0,1},{1,2},{2,3},{3,4},{4,5},{5,6},{6,7},{7,8},{8,9},{9,10},{10,1... | collective-permute-start | bytes 2359304 | tf_op jit(solution)/shard_map/while/body/eval_jaxpr/ppermute | solution.py:20
  849.9 6.0 slice-start
  853.2 2.7 slice-start.1
  859.3 15.6 %collective-permute-start.1 = (bf16[128,1536]{1,0:T(8,128)(2,1)}, bf16[128,1536]{1,0:T(8,128)(2,1)S(1)}, u32[]{:S(2)}, u32[]{:S(2)}) collective-permute-start(bf16[128,1536]{1,0:T(8,128)(2,1)} %get-tuple-element.587), channel_id=1, source_target_pairs={{0,32},{32,64},{64,96},{96,128},{128,160},{160,192},{192,224},{1,3... | collective-permute-start | bytes 1179656 | tf_op jit(solution)/shard_map/while/body/eval_jaxpr/ppermute | solution.py:26
  895.2 14.4 %collective-permute-start = (bf16[128,3072]{1,0:T(8,128)(2,1)}, bf16[128,3072]{1,0:T(8,128)(2,1)S(1)}, u32[]{:S(2)}, u32[]{:S(2)}) collective-permute-start(bf16[128,3072]{1,0:T(8,128)(2,1)} %get-tuple-element.585), channel_id=1, source_target_pairs={{0,1},{1,2},{2,3},{3,4},{4,5},{5,6},{6,7},{7,8},{8,9},{9,10},{10,1... | collective-permute-start | bytes 2359304 | tf_op jit(solution)/shard_map/while/body/eval_jaxpr/ppermute | solution.py:20
  926.8 6.0 slice-start
  930.1 2.7 slice-start.1
  936.2 18.1 %collective-permute-start.1 = (bf16[128,1536]{1,0:T(8,128)(2,1)}, bf16[128,1536]{1,0:T(8,128)(2,1)S(1)}, u32[]{:S(2)}, u32[]{:S(2)}) collective-permute-start(bf16[128,1536]{1,0:T(8,128)(2,1)} %get-tuple-element.587), channel_id=1, source_target_pairs={{0,32},{32,64},{64,96},{96,128},{128,160},{160,192},{192,224},{1,3... | collective-permute-start | bytes 1179656 | tf_op jit(solution)/shard_map/while/body/eval_jaxpr/ppermute | solution.py:26
  974.5 18.3 %collective-permute-start = (bf16[128,3072]{1,0:T(8,128)(2,1)}, bf16[128,3072]{1,0:T(8,128)(2,1)S(1)}, u32[]{:S(2)}, u32[]{:S(2)}) collective-permute-start(bf16[128,3072]{1,0:T(8,128)(2,1)} %get-tuple-element.585), channel_id=1, source_target_pairs={{0,1},{1,2},{2,3},{3,4},{4,5},{5,6},{6,7},{7,8},{8,9},{9,10},{10,1... | collective-permute-start | bytes 2359304 | tf_op jit(solution)/shard_map/while/body/eval_jaxpr/ppermute | solution.py:20
  1010.1 6.0 slice-start
  1013.5 2.7 slice-start.1
  1019.5 3.8 collective-permute-start.1
Sparse Core Ops, SparseCore 0:
  11.2 102.6 all-gather.6
  116.4 125.1 all-gather.4
where the time goes:
time: 1030 us
  waiting for transfers between devices  668 us (65%)
  other arithmetic  126 us (12%)
  local copies, waits for them, and re-layouts  103 us (10%)
  matrix products  82.5 us (8%)
  loops' own time  20.9 us (2%)
  starting transfers between devices  15.9 us (2%)
  between operations  14.1 us (1%)
    ppermute x11, waiting for transfers between devices, shifted_2(): return lax.ppermute(x, axis, pairs)  286 us
    ppermute x12, waiting for transfers between devices, shifted(): return lax.ppermute(value, axis, pairs)  255 us
    all_gather x1, waiting for transfers between devices, on_device(): lax.all_gather(w_qkv[0], 'blk', axis=0, tiled=True)  126 us
    dot_general x4, matrix products, project(): qkv = jnp.dot(modulated, full_qkv, preferred_element_type=jnp.float32)  28.6 us
    dot_general x11, matrix products, slot_step(): jnp.dot(one_hot, modulation_table, precision=lax.Precision.HIGHEST)  26.6 us
    select_n x11, other arithmetic, slot_step(): jnp.where(active, lax.dynamic_update_index_in_dim(own_store, fresh_kv, pa...  25.1 us
    select_n x11, other arithmetic, slot_step(): jnp.where(active, lax.dynamic_update_index_in_dim(near_store, near_fresh,...  24.3 us
    concatenate x4, other arithmetic, attend(): jnp.concatenate([own_rows.reshape(-1, 2 * inner_width), near_rows.reshape...  22.5 us
  transfers between devices with their start and end apart: 25, of which 24 were waited for; matrix products, arithmetic and copies ran while one was open for 5% of the time, Pallas kernels for 0%

commit v1 on v0

--- a/solution.py
+++ b/solution.py
@@ -1,3 +1,4 @@
+import functools
 import math
 import jax
 import jax.numpy as jnp
@@ -12,6 +13,19 @@
 TSTEPS = 16
 TOK_DEV = 128
 NORM_EPS = 1e-06
+
+
+def remake_the_sections(state, across):
+    wide_n = lax.psum(1, axis_name=across)
+    runs = []
+    for p in [*range(state.ndim)]:
+        runs.append(wide_n if p == 0 else 1)
+    return lax.all_to_all(
+        jnp.tile(state, runs), axis_name=across, split_axis=0, concat_axis=0, tiled=True
+    )
+
+
+update_sheet = functools.partial(remake_the_sections, across="blk")
 
 
 def shifted(value, axis, steps):
@@ -47,7 +61,7 @@
     sections = lax.axis_size("section")
     section_id = lax.axis_index("section")
     full_qkv, full_out = (
-        lax.all_gather(w_qkv[0], "blk", axis=0, tiled=True),
+        update_sheet(w_qkv[0]),
         lax.all_gather(w_out[0], "blk", axis=0, tiled=True),
     )
     query_gain = q_gain[0]

time: 1030 us -> 1240 us (1.20)
  waiting for transfers between devices: 668 us -> 843 us
  starting transfers between devices: 15.9 us -> 33.6 us
    ppermute x12, waiting for transfers between devices: 255 us -> 553 us  [shifted(): return lax.ppermute(value, axis, pairs)]
    all_gather x1 -> x0, waiting for transfers between devices: 126 us -> none  [on_device(): lax.all_gather(w_qkv[0], 'blk', axis=0, tiled=True)]
  transfers between devices with their start and end apart: 25 -> 25, of which waited for: 24 -> 23; matrix products, arithmetic and copies ran while one was open for 5% -> 4% of each run, Pallas kernels for 0% -> 0%
where the time goes in v1:
time: 1240 us; the launch traced here: 1230 us
  waiting for transfers between devices  843 us (68%)
  other arithmetic  126 us (10%)
  local copies, waits for them, and re-layouts  110 us (9%)
  matrix products  82.8 us (7%)
  starting transfers between devices  33.6 us (3%)
  loops' own time  23.8 us (2%)
  between operations  14.1 us (1%)
    ppermute x12, waiting for transfers between devices, shifted(): return lax.ppermute(value, axis, pairs)  553 us
    ppermute x11, waiting for transfers between devices, shifted_2(): return lax.ppermute(x, axis, pairs)  289 us
    dot_general x4, matrix products, project(): qkv = jnp.dot(modulated, full_qkv, preferred_element_type=jnp.float32)  28.6 us
    dot_general x11, matrix products, slot_step(): jnp.dot(one_hot, modulation_table, precision=lax.Precision.HIGHEST)  26.8 us
    select_n x11, other arithmetic, slot_step(): jnp.where(active, lax.dynamic_update_index_in_dim(own_store, fresh_kv, pa...  25.1 us
  transfers between devices with their start and end apart: 25, of which 23 were waited for; matrix products, arithmetic and copies ran while one was open for 4% of the time, Pallas kernels for 0%

profile of v1, /device:TPU:7, one launch (start us, length us, event | category | flops | bytes accessed | tf_op | source)
XLA Modules:
  0.0 1233.1 jit_solution(15838335971762245686)
XLA Ops:
  7.2 3.8 copy.63
  11.0 6.7 tile.9
  17.7 11.5 all-to-all-start
  32.2 406.2 %collective-permute-done.2 = bf16[4,128,3072]{2,1,0:T(8,128)(2,1)} collective-permute-done((bf16[4,128,3072]{2,1,0:T(8,128)(2,1)}, bf16[4,128,3072]{2,1,0:T(8,128)(2,1)}, u32[]{:S(2)}, u32[]{:S(2)}) %collective-permute-start.2) | collective-permute-done | bytes 3145760 | tf_op jit(solution)/shard_map/ppermute | solution.py:34
  439.7 786.5 %while.20 = (s32[]{:T(128)}, bf16[128,1536]{1,0:T(8,128)(2,1)S(1)}, bf16[4,128,3072]{2,1,0:T(8,128)(2,1)}, bf16[4,128,3072]{2,1,0:T(8,128)(2,1)}, bf16[4,128,153...) while((s32[]{:T(128)}, bf16[128,1536]{1,0:T(8,128)(2,1)S(1)}, ...), condition=%wide.region_11.12_spmd, body=%wide.region_0.11_spmd.sunk | while | flops 3260855808 | bytes 107183792 | solution.py:174
  446.9 2.8 conditional.4
  451.9 18.9 %collective-permute-done = bf16[128,3072]{1,0:T(8,128)(2,1)S(1)} collective-permute-done((bf16[128,3072]{1,0:T(8,128)(2,1)}, bf16[128,3072]{1,0:T(8,128)(2,1)S(1)}, u32[]{:S(2)}, u32[]{:S(2)}) %collective-permute-start) | collective-permute-done | bytes 786464 | tf_op jit(solution)/shard_map/while/body/eval_jaxpr/ppermute | solution.py:34
  477.7 2.6 collective-permute-done.1
  487.2 2.8 conditional.4
  490.0 6.8 collective-permute-start
  499.0 7.1 collective-permute-done
  513.0 14.5 %collective-permute-done.1 = bf16[128,1536]{1,0:T(8,128)(2,1)S(1)} collective-permute-done((bf16[128,1536]{1,0:T(8,128)(2,1)}, bf16[128,1536]{1,0:T(8,128)(2,1)S(1)}, u32[]{:S(2)}, u32[]{:S(2)}) %collective-permute-start.1) | collective-permute-done | bytes 393248 | tf_op jit(solution)/shard_map/while/body/eval_jaxpr/ppermute | solution.py:40
  534.3 2.8 conditional.4
  539.4 14.2 %collective-permute-done = bf16[128,3072]{1,0:T(8,128)(2,1)S(1)} collective-permute-done((bf16[128,3072]{1,0:T(8,128)(2,1)}, bf16[128,3072]{1,0:T(8,128)(2,1)S(1)}, u32[]{:S(2)}, u32[]{:S(2)}) %collective-permute-start) | collective-permute-done | bytes 786464 | tf_op jit(solution)/shard_map/while/body/eval_jaxpr/ppermute | solution.py:34
  560.4 7.3 collective-permute-done.1
  574.7 2.8 conditional.4
  579.7 14.4 %collective-permute-done = bf16[128,3072]{1,0:T(8,128)(2,1)S(1)} collective-permute-done((bf16[128,3072]{1,0:T(8,128)(2,1)}, bf16[128,3072]{1,0:T(8,128)(2,1)S(1)}, u32[]{:S(2)}, u32[]{:S(2)}) %collective-permute-start) | collective-permute-done | bytes 786464 | tf_op jit(solution)/shard_map/while/body/eval_jaxpr/ppermute | solution.py:34
  601.0 7.1 collective-permute-done.1
  615.0 2.8 conditional.4
  620.0 14.4 %collective-permute-done = bf16[128,3072]{1,0:T(8,128)(2,1)S(1)} collective-permute-done((bf16[128,3072]{1,0:T(8,128)(2,1)}, bf16[128,3072]{1,0:T(8,128)(2,1)S(1)}, u32[]{:S(2)}, u32[]{:S(2)}) %collective-permute-start) | collective-permute-done | bytes 786464 | tf_op jit(solution)/shard_map/while/body/eval_jaxpr/ppermute | solution.py:34
  641.3 7.1 collective-permute-done.1
  651.8 2.4 convolution_reduce_fusion.2
  655.3 2.8 conditional.4
  660.3 14.4 %collective-permute-done = bf16[128,3072]{1,0:T(8,128)(2,1)S(1)} collective-permute-done((bf16[128,3072]{1,0:T(8,128)(2,1)}, bf16[128,3072]{1,0:T(8,128)(2,1)S(1)}, u32[]{:S(2)}, u32[]{:S(2)}) %collective-permute-start) | collective-permute-done | bytes 786464 | tf_op jit(solution)/shard_map/while/body/eval_jaxpr/ppermute | solution.py:34
  681.6 7.1 collective-permute-done.1
  692.2 2.4 convolution_reduce_fusion.2
  695.6 2.8 conditional.4
  700.7 12.2 collective-permute-done
  719.8 205.2 %collective-permute-done.1 = bf16[128,1536]{1,0:T(8,128)(2,1)S(1)} collective-permute-done((bf16[128,1536]{1,0:T(8,128)(2,1)}, bf16[128,1536]{1,0:T(8,128)(2,1)S(1)}, u32[]{:S(2)}, u32[]{:S(2)}) %collective-permute-start.1) | collective-permute-done | bytes 393248 | tf_op jit(solution)/shard_map/while/body/eval_jaxpr/ppermute | solution.py:40
  931.8 13.7 %conditional.4 = (bf16[128,12,128]{0,2,1:T(8,128)(2,1)}, bf16[128,3072]{1,0:T(8,128)(2,1)}, bf16[1,128,3072]{2,1,0:T(8,128)(2,1)}) conditional(s32[]{:T(128)} %convert_element_type.92, () %tuple.70, (bf16[128,1536]{1,0:T(8,128)(2,1)S(1)}, f32[4608]{0:T(1024)}, bf16[1536,4608]{1,0:T(8,128)(2,1)}, f32[1,128]{1,0:T(1,128)S(1)}) %tuple.71), branch_computations={%region_2.2_spmd, %region_3.6_spmd} | conditional | flops 1815284864 | bytes 26018840 | solution.py:117
  933.0 7.2 fusion.6
  948.0 11.9 collective-permute-done
  962.1 24.4 %conditional.5 = (bf16[128,1536]{1,0:T(8,128)(2,1)}, bf16[1,128,1536]{2,1,0:T(8,128)(2,1)}) conditional(s32[]{:T(128)} %convert_element_type.92, () %tuple.69, (bf16[128,1536]{1,0:T(8,128)(2,1)S(1)}, f32[4608]{0:T(1024)}, bf16[4,128,3072]{2,1,0:T(8,128)(2,1)}, bf16[4,128,3072]{2,1,0:T(8,128)(2,1)}, f32[1,128]{1,0:T(1,128)S(1)}, ...), branch_computations={%region_7.7_spmd, %region_8.10_spmd} | conditional | flops 1443506688 | bytes 69053088 | solution.py:164
  962.1 3.2 copy.32
  965.3 4.7 copy.31
  970.0 5.6 pad_maximum_fusion
  977.2 3.3 bitcast_reduce_fusion
  989.8 10.3 collective-permute-done.1
  1007.0 13.7 %conditional.4 = (bf16[128,12,128]{0,2,1:T(8,128)(2,1)}, bf16[128,3072]{1,0:T(8,128)(2,1)}, bf16[1,128,3072]{2,1,0:T(8,128)(2,1)}) conditional(s32[]{:T(128)} %convert_element_type.92, () %tuple.70, (bf16[128,1536]{1,0:T(8,128)(2,1)S(1)}, f32[4608]{0:T(1024)}, bf16[1536,4608]{1,0:T(8,128)(2,1)}, f32[1,128]{1,0:T(1,128)S(1)}) %tuple.71), branch_computations={%region_2.2_spmd, %region_3.6_spmd} | conditional | flops 1815284864 | bytes 26018840 | solution.py:117
  1008.2 7.1 fusion.6
  1023.1 11.9 collective-permute-done
  1037.3 24.4 %conditional.5 = (bf16[128,1536]{1,0:T(8,128)(2,1)}, bf16[1,128,1536]{2,1,0:T(8,128)(2,1)}) conditional(s32[]{:T(128)} %convert_element_type.92, () %tuple.69, (bf16[128,1536]{1,0:T(8,128)(2,1)S(1)}, f32[4608]{0:T(1024)}, bf16[4,128,3072]{2,1,0:T(8,128)(2,1)}, bf16[4,128,3072]{2,1,0:T(8,128)(2,1)}, f32[1,128]{1,0:T(1,128)S(1)}, ...), branch_computations={%region_7.7_spmd, %region_8.10_spmd} | conditional | flops 1443506688 | bytes 69053088 | solution.py:164
  1037.3 3.2 copy.32
  1040.5 4.7 copy.31
  1045.2 5.6 pad_maximum_fusion
  1052.3 3.3 bitcast_reduce_fusion
  1064.9 12.3 collective-permute-done.1
  1084.1 13.7 %conditional.4 = (bf16[128,12,128]{0,2,1:T(8,128)(2,1)}, bf16[128,3072]{1,0:T(8,128)(2,1)}, bf16[1,128,3072]{2,1,0:T(8,128)(2,1)}) conditional(s32[]{:T(128)} %convert_element_type.92, () %tuple.70, (bf16[128,1536]{1,0:T(8,128)(2,1)S(1)}, f32[4608]{0:T(1024)}, bf16[1536,4608]{1,0:T(8,128)(2,1)}, f32[1,128]{1,0:T(1,128)S(1)}) %tuple.71), branch_computations={%region_2.2_spmd, %region_3.6_spmd} | conditional | flops 1815284864 | bytes 26018840 | solution.py:117
  1085.3 7.1 fusion.6
  1100.2 11.9 collective-permute-done
  1114.4 24.4 %conditional.5 = (bf16[128,1536]{1,0:T(8,128)(2,1)}, bf16[1,128,1536]{2,1,0:T(8,128)(2,1)}) conditional(s32[]{:T(128)} %convert_element_type.92, () %tuple.69, (bf16[128,1536]{1,0:T(8,128)(2,1)S(1)}, f32[4608]{0:T(1024)}, bf16[4,128,3072]{2,1,0:T(8,128)(2,1)}, bf16[4,128,3072]{2,1,0:T(8,128)(2,1)}, f32[1,128]{1,0:T(1,128)S(1)}, ...), branch_computations={%region_7.7_spmd, %region_8.10_spmd} | conditional | flops 1443506688 | bytes 69053088 | solution.py:164
  1114.4 3.2 copy.32
  1117.6 4.7 copy.31
  1122.3 5.6 pad_maximum_fusion
  1129.4 3.3 bitcast_reduce_fusion
  1142.0 14.9 %collective-permute-done.1 = bf16[128,1536]{1,0:T(8,128)(2,1)S(1)} collective-permute-done((bf16[128,1536]{1,0:T(8,128)(2,1)}, bf16[128,1536]{1,0:T(8,128)(2,1)S(1)}, u32[]{:S(2)}, u32[]{:S(2)}) %collective-permute-start.1) | collective-permute-done | bytes 393248 | tf_op jit(solution)/shard_map/while/body/eval_jaxpr/ppermute | solution.py:40
  1163.8 13.7 %conditional.4 = (bf16[128,12,128]{0,2,1:T(8,128)(2,1)}, bf16[128,3072]{1,0:T(8,128)(2,1)}, bf16[1,128,3072]{2,1,0:T(8,128)(2,1)}) conditional(s32[]{:T(128)} %convert_element_type.92, () %tuple.70, (bf16[128,1536]{1,0:T(8,128)(2,1)S(1)}, f32[4608]{0:T(1024)}, bf16[1536,4608]{1,0:T(8,128)(2,1)}, f32[1,128]{1,0:T(1,128)S(1)}) %tuple.71), branch_computations={%region_2.2_spmd, %region_3.6_spmd} | conditional | flops 1815284864 | bytes 26018840 | solution.py:117
  1165.0 7.1 fusion.6
  1179.9 15.9 %collective-permute-done = bf16[128,3072]{1,0:T(8,128)(2,1)S(1)} collective-permute-done((bf16[128,3072]{1,0:T(8,128)(2,1)}, bf16[128,3072]{1,0:T(8,128)(2,1)S(1)}, u32[]{:S(2)}, u32[]{:S(2)}) %collective-permute-start) | collective-permute-done | bytes 786464 | tf_op jit(solution)/shard_map/while/body/eval_jaxpr/ppermute | solution.py:34
  1198.1 24.4 %conditional.5 = (bf16[128,1536]{1,0:T(8,128)(2,1)}, bf16[1,128,1536]{2,1,0:T(8,128)(2,1)}) conditional(s32[]{:T(128)} %convert_element_type.92, () %tuple.69, (bf16[128,1536]{1,0:T(8,128)(2,1)S(1)}, f32[4608]{0:T(1024)}, bf16[4,128,3072]{2,1,0:T(8,128)(2,1)}, bf16[4,128,3072]{2,1,0:T(8,128)(2,1)}, f32[1,128]{1,0:T(1,128)S(1)}, ...), branch_computations={%region_7.7_spmd, %region_8.10_spmd} | conditional | flops 1443506688 | bytes 69053088 | solution.py:164
  1198.1 3.2 copy.32
  1201.2 4.7 copy.31
  1205.9 5.6 pad_maximum_fusion
  1213.1 3.3 bitcast_reduce_fusion
  (260 shorter events, 235.2 us)
Async XLA Ops:
  7.2 3.8 copy-start
  17.7 13.5 %copy-start.1 = (f32[1,16,3,1536]{3,1,2,0:T(8,128)S(1)}, f32[1,16,3,1536]{3,1,2,0:T(8,128)}, u32[]{:S(2)}) copy-start(f32[1,16,3,1536]{3,1,2,0:T(8,128)} %param.22) | copy-start | bytes 884740
  17.7 420.7 %all-to-all-start = ((bf16[32,48,4608]{2,1,0:T(8,128)(2,1)}), bf16[32,48,4608]{2,1,0:T(8,128)(2,1)}, u32[]{:S(2)}, u32[]{:S(2)}) async-start(bf16[32,48,4608]{2,1,0:T(8,128)(2,1)} %tile.9), calls=%async_computation | async-start | bytes 28311552 | tf_op jit(solution)/shard_map/all_to_all | solution.py:23
  29.2 410.6 %copy-start.2 = (f32[1,128]{1,0:T(1,128)S(1)}, f32[1,128]{1,0:T(1,128)}, u32[]{:S(2)}) copy-start(f32[1,128]{1,0:T(1,128)} %param.20) | copy-start | bytes 1540
  29.2 410.6 %copy-start.3 = (s32[4]{0:T(128)S(1)}, s32[4]{0:T(128)}, u32[]{:S(2)}) copy-start(s32[4]{0:T(128)} %param.25) | copy-start | bytes 52
  29.2 410.5 %copy-start.4 = (s32[4]{0:T(128)S(1)}, s32[4]{0:T(128)}, u32[]{:S(2)}) copy-start(s32[4]{0:T(128)} %param.24) | copy-start | bytes 52
  29.2 410.5 %copy-start.5 = (f32[1,128]{1,0:T(1,128)S(1)}, f32[1,128]{1,0:T(1,128)}, u32[]{:S(2)}) copy-start(f32[1,128]{1,0:T(1,128)} %param.21) | copy-start | bytes 1540
  29.2 409.2 %all-gather.3.cloned.1.call-start = ((), (), s32[]{:S(2)}) async-start(), calls=%async_computation.1 | async-start | bytes 4866048 | tf_op jit(solution)/shard_map/all_gather | solution.py:65
  29.9 408.5 %collective-permute-start.2 = (bf16[4,128,3072]{2,1,0:T(8,128)(2,1)}, bf16[4,128,3072]{2,1,0:T(8,128)(2,1)}, u32[]{:S(2)}, u32[]{:S(2)}) collective-permute-start(bf16[4,128,3072]{2,1,0:T(8,128)(2,1)} %bitcast.20), channel_id=1, source_target_pairs={{0,1},{1,2},{2,3},{3,4},{4,5},{5,6},{6,7},{7,8},{8,9},{9,10},{10,1... | collective-permute-start | bytes 9437192 | tf_op jit(solution)/shard_map/ppermute | solution.py:34
  449.7 21.1 %collective-permute-start = (bf16[128,3072]{1,0:T(8,128)(2,1)}, bf16[128,3072]{1,0:T(8,128)(2,1)S(1)}, u32[]{:S(2)}, u32[]{:S(2)}) collective-permute-start(bf16[128,3072]{1,0:T(8,128)(2,1)} %get-tuple-element.585), channel_id=1, source_target_pairs={{0,1},{1,2},{2,3},{3,4},{4,5},{5,6},{6,7},{7,8},{8,9},{9,10},{10,1... | collective-permute-start | bytes 2359304 | tf_op jit(solution)/shard_map/while/body/eval_jaxpr/ppermute | solution.py:34
  474.6 5.7 collective-permute-start.1
  490.0 16.0 %collective-permute-start = (bf16[128,3072]{1,0:T(8,128)(2,1)}, bf16[128,3072]{1,0:T(8,128)(2,1)S(1)}, u32[]{:S(2)}, u32[]{:S(2)}) collective-permute-start(bf16[128,3072]{1,0:T(8,128)(2,1)} %get-tuple-element.585), channel_id=1, source_target_pairs={{0,1},{1,2},{2,3},{3,4},{4,5},{5,6},{6,7},{7,8},{8,9},{9,10},{10,1... | collective-permute-start | bytes 2359304 | tf_op jit(solution)/shard_map/while/body/eval_jaxpr/ppermute | solution.py:34
  509.8 17.6 %collective-permute-start.1 = (bf16[128,1536]{1,0:T(8,128)(2,1)}, bf16[128,1536]{1,0:T(8,128)(2,1)S(1)}, u32[]{:S(2)}, u32[]{:S(2)}) collective-permute-start(bf16[128,1536]{1,0:T(8,128)(2,1)} %get-tuple-element.587), channel_id=1, source_target_pairs={{0,32},{32,64},{64,96},{96,128},{128,160},{160,192},{192,224},{1,3... | collective-permute-start | bytes 1179656 | tf_op jit(solution)/shard_map/while/body/eval_jaxpr/ppermute | solution.py:40
  537.2 16.4 %collective-permute-start = (bf16[128,3072]{1,0:T(8,128)(2,1)}, bf16[128,3072]{1,0:T(8,128)(2,1)S(1)}, u32[]{:S(2)}, u32[]{:S(2)}) collective-permute-start(bf16[128,3072]{1,0:T(8,128)(2,1)} %get-tuple-element.585), channel_id=1, source_target_pairs={{0,1},{1,2},{2,3},{3,4},{4,5},{5,6},{6,7},{7,8},{8,9},{9,10},{10,1... | collective-permute-start | bytes 2359304 | tf_op jit(solution)/shard_map/while/body/eval_jaxpr/ppermute | solution.py:34
  557.3 10.4 collective-permute-start.1
  577.5 16.6 %collective-permute-start = (bf16[128,3072]{1,0:T(8,128)(2,1)}, bf16[128,3072]{1,0:T(8,128)(2,1)S(1)}, u32[]{:S(2)}, u32[]{:S(2)}) collective-permute-start(bf16[128,3072]{1,0:T(8,128)(2,1)} %get-tuple-element.585), channel_id=1, source_target_pairs={{0,1},{1,2},{2,3},{3,4},{4,5},{5,6},{6,7},{7,8},{8,9},{9,10},{10,1... | collective-permute-start | bytes 2359304 | tf_op jit(solution)/shard_map/while/body/eval_jaxpr/ppermute | solution.py:34
  597.9 10.2 collective-permute-start.1
  617.8 16.6 %collective-permute-start = (bf16[128,3072]{1,0:T(8,128)(2,1)}, bf16[128,3072]{1,0:T(8,128)(2,1)S(1)}, u32[]{:S(2)}, u32[]{:S(2)}) collective-permute-start(bf16[128,3072]{1,0:T(8,128)(2,1)} %get-tuple-element.585), channel_id=1, source_target_pairs={{0,1},{1,2},{2,3},{3,4},{4,5},{5,6},{6,7},{7,8},{8,9},{9,10},{10,1... | collective-permute-start | bytes 2359304 | tf_op jit(solution)/shard_map/while/body/eval_jaxpr/ppermute | solution.py:34
  638.2 10.2 collective-permute-start.1
  658.1 16.6 %collective-permute-start = (bf16[128,3072]{1,0:T(8,128)(2,1)}, bf16[128,3072]{1,0:T(8,128)(2,1)S(1)}, u32[]{:S(2)}, u32[]{:S(2)}) collective-permute-start(bf16[128,3072]{1,0:T(8,128)(2,1)} %get-tuple-element.585), channel_id=1, source_target_pairs={{0,1},{1,2},{2,3},{3,4},{4,5},{5,6},{6,7},{7,8},{8,9},{9,10},{10,1... | collective-permute-start | bytes 2359304 | tf_op jit(solution)/shard_map/while/body/eval_jaxpr/ppermute | solution.py:34
  678.5 10.2 collective-permute-start.1
  698.5 14.4 %collective-permute-start = (bf16[128,3072]{1,0:T(8,128)(2,1)}, bf16[128,3072]{1,0:T(8,128)(2,1)S(1)}, u32[]{:S(2)}, u32[]{:S(2)}) collective-permute-start(bf16[128,3072]{1,0:T(8,128)(2,1)} %get-tuple-element.585), channel_id=1, source_target_pairs={{0,1},{1,2},{2,3},{3,4},{4,5},{5,6},{6,7},{7,8},{8,9},{9,10},{10,1... | collective-permute-start | bytes 2359304 | tf_op jit(solution)/shard_map/while/body/eval_jaxpr/ppermute | solution.py:34
  716.6 208.3 %collective-permute-start.1 = (bf16[128,1536]{1,0:T(8,128)(2,1)}, bf16[128,1536]{1,0:T(8,128)(2,1)S(1)}, u32[]{:S(2)}, u32[]{:S(2)}) collective-permute-start(bf16[128,1536]{1,0:T(8,128)(2,1)} %get-tuple-element.587), channel_id=1, source_target_pairs={{0,32},{32,64},{64,96},{96,128},{128,160},{160,192},{192,224},{1,3... | collective-permute-start | bytes 1179656 | tf_op jit(solution)/shard_map/while/body/eval_jaxpr/ppermute | solution.py:40
  945.5 14.4 %collective-permute-start = (bf16[128,3072]{1,0:T(8,128)(2,1)}, bf16[128,3072]{1,0:T(8,128)(2,1)S(1)}, u32[]{:S(2)}, u32[]{:S(2)}) collective-permute-start(bf16[128,3072]{1,0:T(8,128)(2,1)} %get-tuple-element.585), channel_id=1, source_target_pairs={{0,1},{1,2},{2,3},{3,4},{4,5},{5,6},{6,7},{7,8},{8,9},{9,10},{10,1... | collective-permute-start | bytes 2359304 | tf_op jit(solution)/shard_map/while/body/eval_jaxpr/ppermute | solution.py:34
  977.2 6.0 slice-start
  980.5 2.7 slice-start.1
  986.5 13.5 %collective-permute-start.1 = (bf16[128,1536]{1,0:T(8,128)(2,1)}, bf16[128,1536]{1,0:T(8,128)(2,1)S(1)}, u32[]{:S(2)}, u32[]{:S(2)}) collective-permute-start(bf16[128,1536]{1,0:T(8,128)(2,1)} %get-tuple-element.587), channel_id=1, source_target_pairs={{0,32},{32,64},{64,96},{96,128},{128,160},{160,192},{192,224},{1,3... | collective-permute-start | bytes 1179656 | tf_op jit(solution)/shard_map/while/body/eval_jaxpr/ppermute | solution.py:40
  1020.7 14.4 %collective-permute-start = (bf16[128,3072]{1,0:T(8,128)(2,1)}, bf16[128,3072]{1,0:T(8,128)(2,1)S(1)}, u32[]{:S(2)}, u32[]{:S(2)}) collective-permute-start(bf16[128,3072]{1,0:T(8,128)(2,1)} %get-tuple-element.585), channel_id=1, source_target_pairs={{0,1},{1,2},{2,3},{3,4},{4,5},{5,6},{6,7},{7,8},{8,9},{9,10},{10,1... | collective-permute-start | bytes 2359304 | tf_op jit(solution)/shard_map/while/body/eval_jaxpr/ppermute | solution.py:34
  1052.3 6.0 slice-start
  1055.6 2.7 slice-start.1
  1061.7 15.5 %collective-permute-start.1 = (bf16[128,1536]{1,0:T(8,128)(2,1)}, bf16[128,1536]{1,0:T(8,128)(2,1)S(1)}, u32[]{:S(2)}, u32[]{:S(2)}) collective-permute-start(bf16[128,1536]{1,0:T(8,128)(2,1)} %get-tuple-element.587), channel_id=1, source_target_pairs={{0,32},{32,64},{64,96},{96,128},{128,160},{160,192},{192,224},{1,3... | collective-permute-start | bytes 1179656 | tf_op jit(solution)/shard_map/while/body/eval_jaxpr/ppermute | solution.py:40
  1097.8 14.4 %collective-permute-start = (bf16[128,3072]{1,0:T(8,128)(2,1)}, bf16[128,3072]{1,0:T(8,128)(2,1)S(1)}, u32[]{:S(2)}, u32[]{:S(2)}) collective-permute-start(bf16[128,3072]{1,0:T(8,128)(2,1)} %get-tuple-element.585), channel_id=1, source_target_pairs={{0,1},{1,2},{2,3},{3,4},{4,5},{5,6},{6,7},{7,8},{8,9},{9,10},{10,1... | collective-permute-start | bytes 2359304 | tf_op jit(solution)/shard_map/while/body/eval_jaxpr/ppermute | solution.py:34
  1129.4 6.0 slice-start
  1132.7 2.7 slice-start.1
  1138.8 18.1 %collective-permute-start.1 = (bf16[128,1536]{1,0:T(8,128)(2,1)}, bf16[128,1536]{1,0:T(8,128)(2,1)S(1)}, u32[]{:S(2)}, u32[]{:S(2)}) collective-permute-start(bf16[128,1536]{1,0:T(8,128)(2,1)} %get-tuple-element.587), channel_id=1, source_target_pairs={{0,32},{32,64},{64,96},{96,128},{128,160},{160,192},{192,224},{1,3... | collective-permute-start | bytes 1179656 | tf_op jit(solution)/shard_map/while/body/eval_jaxpr/ppermute | solution.py:40
  1177.5 18.3 %collective-permute-start = (bf16[128,3072]{1,0:T(8,128)(2,1)}, bf16[128,3072]{1,0:T(8,128)(2,1)S(1)}, u32[]{:S(2)}, u32[]{:S(2)}) collective-permute-start(bf16[128,3072]{1,0:T(8,128)(2,1)} %get-tuple-element.585), channel_id=1, source_target_pairs={{0,1},{1,2},{2,3},{3,4},{4,5},{5,6},{6,7},{7,8},{8,9},{9,10},{10,1... | collective-permute-start | bytes 2359304 | tf_op jit(solution)/shard_map/while/body/eval_jaxpr/ppermute | solution.py:34
  1213.1 6.0 slice-start
  1216.4 2.7 slice-start.1
  1222.5 3.8 collective-permute-start.1
Sparse Core Ops, SparseCore 0:
  32.6 156.9 all-gather.2
